TPU v7x, 128 devices: a whole 4x4x4 slice. The times are simulated.
128 devices in a mesh: grp: 4 (over y), dev: 32 (over z, x, core).
Axes of the slice: x: 4, y: 4, z: 4, core: 2. Of those that a mesh axis runs over, the one named last changes fastest.
Arguments:
- integral_slabs: bfloat16 [32, 512, 512], P('dev'), may hold values from -6 to 6
- slab_owner: int32 [32], replicated, may hold values from 0 to 31, each once
- pair_orbs: int32 [1024, 2], P(('grp', 'dev')), may hold values from 0 to 31, all different within a row; in each aligned block of 8 rows (0 to 7, 8 to 15, ...) at most 2 rows name the same one
- domain_bases: bfloat16 [1024, 512, 128], P(('grp', 'dev')), may hold values from -0.25 to 0.25
- amplitudes: bfloat16 [1024, 128, 128], P(('grp', 'dev')), may hold values from -6 to 6
- coupled: int32 [1024, 32], P(('grp', 'dev')), may hold values from 0 to 31
- coupled_len: int32 [1024], P(('grp', 'dev')), may hold values from 1 to 32, as said below
Outputs:
- residual: float32 [1024, 128, 128], P(('grp', 'dev'))
Inputs may be any that keep to these rules, and one draw needn't show every extreme that they name: `slab_owner`: a permutation of the positions. `pair_orbs`: the two orbitals of a pair differ; among the pairs of one device no orbital is named more than 2 times. `coupled_len`: pair 0 uses all 32 slots.
All inputs are finite; a program needn't handle non-finite values.
Results may differ from a plain program's by a relative error of at most 0.005.
Values may be sent and summed in bfloat16 or wider, within the bound.
A program may use at most 128 MiB of HBM per device.

v0:
```python
import math
import jax
import jax.numpy as jnp
from jax import lax
from jax.sharding import PartitionSpec as P

NAUX = 512
NORB = 512
NPNO = 128


def side_positions(orbitals, slab_owner):
    flat = orbitals.reshape(-1)
    table = jnp.arange(slab_owner.shape[0], dtype=jnp.int32)
    return jnp.sum(jnp.where(flat[:, None] == table[None, :], slab_owner[None, :], 0), axis=1)


def make_fold(positions, slab_piece):
    rows = jnp.arange(slab_piece.shape[0], dtype=jnp.int32)
    select = (positions[:, None] == rows[None, :]).astype(jnp.bfloat16)
    picked = jnp.einsum("sk,kxn->sxn", select, slab_piece, preferred_element_type=jnp.float32)
    return picked.astype(jnp.bfloat16)


def half_pairs(halves):
    pair_count = halves.shape[0] // 2
    paired = halves.reshape(pair_count, 2, halves.shape[1], halves.shape[2])
    inverse_root = 1.0 / math.sqrt(NAUX)
    return (
        jnp.einsum("pan,pam->pnm", paired[:, 0], paired[:, 1], preferred_element_type=jnp.float32)
        * inverse_root
    )


def coupled_part(domain_bases, coupled, coupled_len, cand_bases, cand_amps):
    cand_count = cand_bases.shape[0]
    slot_live = (jnp.arange(coupled.shape[1])[None, :] < coupled_len[:, None]).astype(jnp.float32)
    matches = (
        coupled[:, :, None] == jnp.arange(cand_count, dtype=jnp.int32)[None, None, :]
    ).astype(jnp.float32)
    counts = jnp.einsum("ps,psc->pc", slot_live, matches)

    def one_pair(inputs):
        domain_basis, weights = inputs
        intersection = jnp.einsum(
            "ra,crb->cab", domain_basis, cand_bases, preferred_element_type=jnp.float32
        ).astype(jnp.bfloat16)
        projected = jnp.einsum(
            "cab,cbd->cad", intersection, cand_amps, preferred_element_type=jnp.float32
        ).astype(jnp.bfloat16)
        coupled_terms = jnp.einsum(
            "cad,ced->cae", projected, intersection, preferred_element_type=jnp.float32
        )
        return jnp.einsum("c,cae->ae", weights, coupled_terms)

    return lax.map(one_pair, (domain_bases, counts))


def on_device(
    integral_slabs, slab_owner, pair_orbs, domain_bases, amplitudes, coupled, coupled_len
):
    naux_full = integral_slabs.shape[1]
    norb_full = integral_slabs.shape[2]
    npno = domain_bases.shape[2]
    pair_count = domain_bases.shape[0]
    cand_bases, cand_amps = (
        lax.all_gather(domain_bases, "grp", axis=0, tiled=True),
        lax.all_gather(amplitudes, "grp", axis=0, tiled=True),
    )
    positions = side_positions(pair_orbs, slab_owner)
    side_slabs = make_fold(positions, lax.all_gather(integral_slabs, "dev", axis=0, tiled=True))
    paired_slabs = side_slabs.reshape(pair_count, 2, naux_full, norb_full)
    halves = jnp.einsum(
        "pkxn,pnq->pkxq", paired_slabs, domain_bases, preferred_element_type=jnp.float32
    ).astype(jnp.bfloat16)
    halves = halves.reshape(2 * pair_count, naux_full, npno)
    exchange = half_pairs(halves)
    coupled_sum = coupled_part(domain_bases, coupled, coupled_len, cand_bases, cand_amps)
    return exchange + NORB / NPNO * coupled_sum


def solution(mesh):
    in_specs = (
        P("dev", None, None),
        P(),
        P(("grp", "dev"), None),
        P(("grp", "dev"), None, None),
        P(("grp", "dev"), None, None),
        P(("grp", "dev"), None),
        P(("grp", "dev")),
    )
    out_specs = P(("grp", "dev"), None, None)
    return jax.shard_map(
        on_device, mesh=mesh, in_specs=in_specs, out_specs=out_specs, check_vma=False
    )
```

profile of v0, /device:TPU:1, one launch (start us, length us, event | category | flops | bytes accessed | tf_op | source)
XLA Modules:
  0.0 207.8 jit_solution(17346117150356649458)
XLA Ops:
  12.1 22.2 %all-gather.8.cloned.1.call-done = bf16[32,128,128]{2,1,0:T(8,128)(2,1)} async-done(((bf16[8,128,128]{2,1,0:T(8,128)(2,1)}), bf16[32,128,128]{2,1,0:T(8,128)(2,1)}) %all-gather.8.cloned.1.call-update) | async-done | bytes 1048592 | tf_op jit(solution)/shard_map/all_gather | solution.py:68
  34.3 52.2 %all-gather.6.cloned.1.call-done = bf16[32,512,128]{2,1,0:T(8,128)(2,1)} async-done(((bf16[8,512,128]{2,1,0:T(8,128)(2,1)}), bf16[32,512,128]{2,1,0:T(8,128)(2,1)}) %all-gather.6.cloned.1.call-update) | async-done | bytes 4194320 | tf_op jit(solution)/shard_map/all_gather | solution.py:67
  86.4 49.6 %while.10 = (s32[]{:T(128)}, f32[8,128,128]{2,1,0:T(8,128)S(1)}, bf16[8,32]{1,0:T(8,128)(2,1)S(1)}, bf16[8,512,128]{2,1,0:T(8,128)(2,1)}, bf16[32,512,128]{2,1,0...) while((s32[]{:T(128)}, f32[8,128,128]{2,1,0:T(8,128)S(1)}, bf16[8,32]{1,0:T(8,128)(2,1)S(1)}, ...), condition=%wide.region_2.3_spmd, body=%wide.region_1.2_spmd.sunk | while | flops 807403520 | bytes 9765973 | solution.py:56
  86.4 3.0 %fusion.45 = bf16[32,128,128]{2,1,0:T(8,128)(2,1)S(1)} fusion(bf16[32,512,128]{2,1,0:T(8,128)(2,1)} %get-tuple-element.129, bf16[8,512,128]{2,1,0:T(8,128)(2,1)} %get-tuple-element.128, s32[]{:T(128)} %get-tuple-element.118), kind=kOutput, calls=%fused_computation.4.clone.1 | convolution fusion | flops 537395200 | bytes 5374464 | tf_op jit(solution)/shard_map/while/body/eval_jaxpr/ra,crb->cab/dot_general | solution.py:45
  89.4 2.4 %fusion.46 = bf16[32,128,128]{2,1,0:T(8,128)(2,1)S(1)} fusion(bf16[32,128,128]{2,1,0:T(8,128)(2,1)S(1)} %fusion.45, bf16[32,128,128]{2,1,0:T(8,128)(2,1)} %get-tuple-element.130), kind=kOutput, calls=%fused_computation.5.clone.1 | convolution fusion | flops 268959744 | bytes 3145728 | tf_op jit(solution)/shard_map/while/body/eval_jaxpr/cad,ced->cae/dot_general | solution.py:51
  92.5 3.0 %fusion.45 = bf16[32,128,128]{2,1,0:T(8,128)(2,1)S(1)} fusion(bf16[32,512,128]{2,1,0:T(8,128)(2,1)} %get-tuple-element.129, bf16[8,512,128]{2,1,0:T(8,128)(2,1)} %get-tuple-element.128, s32[]{:T(128)} %get-tuple-element.118), kind=kOutput, calls=%fused_computation.4.clone.1 | convolution fusion | flops 537395200 | bytes 5374464 | tf_op jit(solution)/shard_map/while/body/eval_jaxpr/ra,crb->cab/dot_general | solution.py:45
  95.5 2.4 %fusion.46 = bf16[32,128,128]{2,1,0:T(8,128)(2,1)S(1)} fusion(bf16[32,128,128]{2,1,0:T(8,128)(2,1)S(1)} %fusion.45, bf16[32,128,128]{2,1,0:T(8,128)(2,1)} %get-tuple-element.130), kind=kOutput, calls=%fused_computation.5.clone.1 | convolution fusion | flops 268959744 | bytes 3145728 | tf_op jit(solution)/shard_map/while/body/eval_jaxpr/cad,ced->cae/dot_general | solution.py:51
  98.6 3.3 %fusion.45 = bf16[32,128,128]{2,1,0:T(8,128)(2,1)S(1)} fusion(bf16[32,512,128]{2,1,0:T(8,128)(2,1)} %get-tuple-element.129, bf16[8,512,128]{2,1,0:T(8,128)(2,1)} %get-tuple-element.128, s32[]{:T(128)} %get-tuple-element.118), kind=kOutput, calls=%fused_computation.4.clone.1 | convolution fusion | flops 537395200 | bytes 5374464 | tf_op jit(solution)/shard_map/while/body/eval_jaxpr/ra,crb->cab/dot_general | solution.py:45
  101.9 2.4 %fusion.46 = bf16[32,128,128]{2,1,0:T(8,128)(2,1)S(1)} fusion(bf16[32,128,128]{2,1,0:T(8,128)(2,1)S(1)} %fusion.45, bf16[32,128,128]{2,1,0:T(8,128)(2,1)} %get-tuple-element.130), kind=kOutput, calls=%fused_computation.5.clone.1 | convolution fusion | flops 268959744 | bytes 3145728 | tf_op jit(solution)/shard_map/while/body/eval_jaxpr/cad,ced->cae/dot_general | solution.py:51
  105.0 3.1 %fusion.45 = bf16[32,128,128]{2,1,0:T(8,128)(2,1)S(1)} fusion(bf16[32,512,128]{2,1,0:T(8,128)(2,1)} %get-tuple-element.129, bf16[8,512,128]{2,1,0:T(8,128)(2,1)} %get-tuple-element.128, s32[]{:T(128)} %get-tuple-element.118), kind=kOutput, calls=%fused_computation.4.clone.1 | convolution fusion | flops 537395200 | bytes 5374464 | tf_op jit(solution)/shard_map/while/body/eval_jaxpr/ra,crb->cab/dot_general | solution.py:45
  108.1 2.4 %fusion.46 = bf16[32,128,128]{2,1,0:T(8,128)(2,1)S(1)} fusion(bf16[32,128,128]{2,1,0:T(8,128)(2,1)S(1)} %fusion.45, bf16[32,128,128]{2,1,0:T(8,128)(2,1)} %get-tuple-element.130), kind=kOutput, calls=%fused_computation.5.clone.1 | convolution fusion | flops 268959744 | bytes 3145728 | tf_op jit(solution)/shard_map/while/body/eval_jaxpr/cad,ced->cae/dot_general | solution.py:51
  111.2 3.0 %fusion.45 = bf16[32,128,128]{2,1,0:T(8,128)(2,1)S(1)} fusion(bf16[32,512,128]{2,1,0:T(8,128)(2,1)} %get-tuple-element.129, bf16[8,512,128]{2,1,0:T(8,128)(2,1)} %get-tuple-element.128, s32[]{:T(128)} %get-tuple-element.118), kind=kOutput, calls=%fused_computation.4.clone.1 | convolution fusion | flops 537395200 | bytes 5374464 | tf_op jit(solution)/shard_map/while/body/eval_jaxpr/ra,crb->cab/dot_general | solution.py:45
  114.2 2.4 %fusion.46 = bf16[32,128,128]{2,1,0:T(8,128)(2,1)S(1)} fusion(bf16[32,128,128]{2,1,0:T(8,128)(2,1)S(1)} %fusion.45, bf16[32,128,128]{2,1,0:T(8,128)(2,1)} %get-tuple-element.130), kind=kOutput, calls=%fused_computation.5.clone.1 | convolution fusion | flops 268959744 | bytes 3145728 | tf_op jit(solution)/shard_map/while/body/eval_jaxpr/cad,ced->cae/dot_general | solution.py:51
  117.3 3.0 %fusion.45 = bf16[32,128,128]{2,1,0:T(8,128)(2,1)S(1)} fusion(bf16[32,512,128]{2,1,0:T(8,128)(2,1)} %get-tuple-element.129, bf16[8,512,128]{2,1,0:T(8,128)(2,1)} %get-tuple-element.128, s32[]{:T(128)} %get-tuple-element.118), kind=kOutput, calls=%fused_computation.4.clone.1 | convolution fusion | flops 537395200 | bytes 5374464 | tf_op jit(solution)/shard_map/while/body/eval_jaxpr/ra,crb->cab/dot_general | solution.py:45
  120.3 2.4 %fusion.46 = bf16[32,128,128]{2,1,0:T(8,128)(2,1)S(1)} fusion(bf16[32,128,128]{2,1,0:T(8,128)(2,1)S(1)} %fusion.45, bf16[32,128,128]{2,1,0:T(8,128)(2,1)} %get-tuple-element.130), kind=kOutput, calls=%fused_computation.5.clone.1 | convolution fusion | flops 268959744 | bytes 3145728 | tf_op jit(solution)/shard_map/while/body/eval_jaxpr/cad,ced->cae/dot_general | solution.py:51
  123.4 3.1 %fusion.45 = bf16[32,128,128]{2,1,0:T(8,128)(2,1)S(1)} fusion(bf16[32,512,128]{2,1,0:T(8,128)(2,1)} %get-tuple-element.129, bf16[8,512,128]{2,1,0:T(8,128)(2,1)} %get-tuple-element.128, s32[]{:T(128)} %get-tuple-element.118), kind=kOutput, calls=%fused_computation.4.clone.1 | convolution fusion | flops 537395200 | bytes 5374464 | tf_op jit(solution)/shard_map/while/body/eval_jaxpr/ra,crb->cab/dot_general | solution.py:45
  126.5 2.4 %fusion.46 = bf16[32,128,128]{2,1,0:T(8,128)(2,1)S(1)} fusion(bf16[32,128,128]{2,1,0:T(8,128)(2,1)S(1)} %fusion.45, bf16[32,128,128]{2,1,0:T(8,128)(2,1)} %get-tuple-element.130), kind=kOutput, calls=%fused_computation.5.clone.1 | convolution fusion | flops 268959744 | bytes 3145728 | tf_op jit(solution)/shard_map/while/body/eval_jaxpr/cad,ced->cae/dot_general | solution.py:51
  129.6 3.1 %fusion.45 = bf16[32,128,128]{2,1,0:T(8,128)(2,1)S(1)} fusion(bf16[32,512,128]{2,1,0:T(8,128)(2,1)} %get-tuple-element.129, bf16[8,512,128]{2,1,0:T(8,128)(2,1)} %get-tuple-element.128, s32[]{:T(128)} %get-tuple-element.118), kind=kOutput, calls=%fused_computation.4.clone.1 | convolution fusion | flops 537395200 | bytes 5374464 | tf_op jit(solution)/shard_map/while/body/eval_jaxpr/ra,crb->cab/dot_general | solution.py:45
  132.7 2.4 %fusion.46 = bf16[32,128,128]{2,1,0:T(8,128)(2,1)S(1)} fusion(bf16[32,128,128]{2,1,0:T(8,128)(2,1)S(1)} %fusion.45, bf16[32,128,128]{2,1,0:T(8,128)(2,1)} %get-tuple-element.130), kind=kOutput, calls=%fused_computation.5.clone.1 | convolution fusion | flops 268959744 | bytes 3145728 | tf_op jit(solution)/shard_map/while/body/eval_jaxpr/cad,ced->cae/dot_general | solution.py:51
  136.0 26.3 %all-gather.4.cloned.1.call-done = bf16[32,512,512]{2,1,0:T(8,128)(2,1)} async-done(((bf16[1,512,512]{2,1,0:T(8,128)(2,1)}), bf16[32,512,512]{2,1,0:T(8,128)(2,1)}) %all-gather.4.cloned.1.call-update) | async-done | bytes 16777232 | tf_op jit(solution)/shard_map/all_gather | solution.py:71
  162.3 20.3 %fusion.11 = bf16[16,512,512]{2,0,1:T(8,128)(2,1)} fusion(bf16[32,512,512]{2,1,0:T(8,128)(2,1)} %all-gather.4.cloned.1.call-done, s32[16]{0:T(128)S(1)} %select_reduce_fusion), kind=kOutput, calls=%fused_computation.14 | convolution fusion | flops 272630272 | bytes 25165888 | tf_op jit(solution)/shard_map/sk,kxn->sxn/dot_general | solution.py:21
  182.6 11.7 %copy.34 = bf16[16,512,512]{2,1,0:T(8,128)(2,1)} copy(bf16[16,512,512]{2,0,1:T(8,128)(2,1)} %fusion.11) | data formatting | bytes 16777216 | tf_op jit(solution)/shard_map/reshape | solution.py:72
  194.2 5.7 %convolution_convert_fusion.2 = bf16[8,2,512,128]{3,2,1,0:T(8,128)(2,1)S(1)} fusion(bf16[8,2,512,512]{3,2,1,0:T(8,128)(2,1)} %bitcast.55, bf16[8,512,128]{2,1,0:T(8,128)(2,1)S(1)} %copy-done), kind=kOutput, calls=%fused_computation.15 | convolution fusion | flops 1074790400 | bytes 11534336 | tf_op jit(solution)/shard_map/pkxn,pnq->pkxq/dot_general | solution.py:73
  200.0 1.3 fusion.14
  (31 shorter events, 10.9 us)
Async XLA Ops:
  6.5 27.7 %all-gather.8.cloned.1.call-start = ((), (), s32[]{:S(2)}) async-start(), calls=%async_computation.2 | async-start | bytes 1310720 | tf_op jit(solution)/shard_map/all_gather | solution.py:68
  7.3 79.2 %all-gather.6.cloned.1.call-start = ((), (), s32[]{:S(2)}) async-start(), calls=%async_computation.1 | async-start | bytes 5242880 | tf_op jit(solution)/shard_map/all_gather | solution.py:67
  8.0 154.3 %all-gather.4.cloned.1.call-start = ((), (), s32[]{:S(2)}) async-start(), calls=%async_computation | async-start | bytes 17301504 | tf_op jit(solution)/shard_map/all_gather | solution.py:71
  182.6 11.7 %copy-start = (bf16[8,512,128]{2,1,0:T(8,128)(2,1)S(1)}, bf16[8,512,128]{2,1,0:T(8,128)(2,1)}, u32[]{:S(2)}) copy-start(bf16[8,512,128]{2,1,0:T(8,128)(2,1)} %get-tuple-element.140) | copy-start | bytes 3145732
Sparse Core Ops, SparseCore 0:
  9.0 25.2 all-gather.7
  35.9 50.4 all-gather.5
  88.7 73.5 all-gather.3
where the time goes:
time: 208 us
  waiting for transfers between devices  103 us (50%)
  matrix products  77.3 us (37%)
  between operations  13.1 us (6%)
  local copies, waits for them, and re-layouts  12.6 us (6%)
    all_gather x1, waiting for transfers between devices, on_device(): lax.all_gather(domain_bases, 'grp', axis=0, tiled=True)  52.2 us
    all_gather x1, waiting for transfers between devices, on_device(): lax.all_gather(integral_slabs, 'dev', axis=0, tiled=True)  26.3 us
    dot_general x8, matrix products, one_pair(): jnp.einsum('ra,crb->cab', domain_basis, cand_bases, preferred_element_typ...  24.7 us
    all_gather x1, waiting for transfers between devices, on_device(): lax.all_gather(amplitudes, 'grp', axis=0, tiled=True)  22.2 us
    dot_general x1, matrix products, make_fold(): jnp.einsum('sk,kxn->sxn', select, slab_piece, preferred_element_type=jnp....  20.3 us
    dot_general x8, matrix products, one_pair(): jnp.einsum('cad,ced->cae', projected, intersection, preferred_element_typ...  19.1 us
    reshape x1, local copies, waits for them, and re-layouts, on_device(): paired_slabs = side_slabs.reshape(pair_count, 2, naux_full, norb_full)  11.7 us
    dot_general x1, matrix products, on_device(): jnp.einsum('pkxn,pnq->pkxq', paired_slabs, domain_bases, preferred_elemen...  5.71 us
  transfers between devices with their start and end apart: 3, of which 3 were waited for; matrix products, arithmetic and copies ran while one was open for 25% of the time, Pallas kernels for 0%

commit v1 on v0

--- a/solution.py
+++ b/solution.py
@@ -65,7 +65,9 @@
     pair_count = domain_bases.shape[0]
     cand_bases, cand_amps = (
         lax.all_gather(domain_bases, "grp", axis=0, tiled=True),
-        lax.all_gather(amplitudes, "grp", axis=0, tiled=True),
+        jnp.concatenate(
+            lax.all_to_all(jnp.stack([amplitudes] * lax.axis_size("grp")), "grp", 0, 0), axis=0
+        ),
     )
     positions = side_positions(pair_orbs, slab_owner)
     side_slabs = make_fold(positions, lax.all_gather(integral_slabs, "dev", axis=0, tiled=True))

time: 208 us -> 187 us (0.90)
  waiting for transfers between devices: 103 us -> 79 us
  matrix products: 77.3 us -> 67.3 us
  local copies, waits for them, and re-layouts: 12.6 us -> 19.8 us
  starting transfers between devices: 0.08 us -> 5.04 us
    all_gather x1 -> x0, waiting for transfers between devices: 22.2 us -> none  [on_device(): lax.all_gather(amplitudes, 'grp', axis=0, tiled=True)]
    all_gather x1, waiting for transfers between devices: 52.2 us -> 32.9 us  [on_device(): lax.all_gather(domain_bases, 'grp', axis=0, tiled=True)]
    all_to_all x0 -> x1, waiting for transfers between devices: none -> 13.4 us  [on_device(): lax.all_to_all(jnp.stack([amplitudes] * lax.axis_size('grp')), 'grp', 0, 0)]
    dot_general x8, matrix products: 19.1 us -> 9.2 us  [one_pair(): jnp.einsum('cad,ced->cae', projected, intersection, preferred_element_typ...]
    all_gather x1, waiting for transfers between devices: 26.3 us -> 31.3 us  [on_device(): lax.all_gather(integral_slabs, 'dev', axis=0, tiled=True)]
    dynamic_update_slice x8, local copies, waits for them, and re-layouts: 0.07 us -> 5.1 us  [coupled_part(): return lax.map(one_pair, (domain_bases, counts))]
    all_to_all x0 -> x1, starting transfers between devices: none -> 5 us  [on_device(): lax.all_to_all(jnp.stack([amplitudes] * lax.axis_size('grp')), 'grp', 0, 0)]
    another operation x0 -> x1, local copies, waits for them, and re-layouts: none -> 2.16 us  [on_device(): jnp.stack([amplitudes] * lax.axis_size('grp'))]
  transfers between devices with their start and end apart: 3 -> 3, of which waited for: 3 -> 3; matrix products, arithmetic and copies ran while one was open for 25% -> 27% of each run, Pallas kernels for 0% -> 0%
where the time goes in v1:
time: 187 us; the launch traced here: 186 us
  waiting for transfers between devices  79 us (42%)
  matrix products  67.3 us (36%)
  local copies, waits for them, and re-layouts  19.8 us (11%)
  between operations  13.4 us (7%)
  starting transfers between devices  5.04 us (3%)
    all_gather x1, waiting for transfers between devices, on_device(): lax.all_gather(domain_bases, 'grp', axis=0, tiled=True)  32.9 us
    all_gather x1, waiting for transfers between devices, on_device(): lax.all_gather(integral_slabs, 'dev', axis=0, tiled=True)  31.3 us
    dot_general x8, matrix products, one_pair(): jnp.einsum('ra,crb->cab', domain_basis, cand_bases, preferred_element_typ...  24.5 us
    dot_general x1, matrix products, make_fold(): jnp.einsum('sk,kxn->sxn', select, slab_piece, preferred_element_type=jnp....  20.3 us
    all_to_all x1, waiting for transfers between devices, on_device(): lax.all_to_all(jnp.stack([amplitudes] * lax.axis_size('grp')), 'grp', 0, 0)  13.4 us
    reshape x1, local copies, waits for them, and re-layouts, on_device(): paired_slabs = side_slabs.reshape(pair_count, 2, naux_full, norb_full)  11.7 us
    dot_general x8, matrix products, one_pair(): jnp.einsum('cad,ced->cae', projected, intersection, preferred_element_typ...  9.2 us
    dot_general x1, matrix products, on_device(): jnp.einsum('pkxn,pnq->pkxq', paired_slabs, domain_bases, preferred_elemen...  5.77 us
  transfers between devices with their start and end apart: 3, of which 3 were waited for; matrix products, arithmetic and copies ran while one was open for 27% of the time, Pallas kernels for 0%

profile of v1, /device:TPU:1, one launch (start us, length us, event | category | flops | bytes accessed | tf_op | source)
XLA Modules:
  0.0 186.2 jit_solution(15276243137111669447)
XLA Ops:
  8.0 2.2 %stack.2 = bf16[4,8,128,128]{3,2,1,0:T(8,128)(2,1)} broadcast(bf16[8,128,128]{2,1,0:T(8,128)(2,1)} %param.13), dimensions={1,2,3} | broadcast | bytes 1310720 | tf_op jit(solution)/shard_map/stack | solution.py:69
  10.2 5.0 %all-to-all-start = ((bf16[4,8,128,128]{3,2,1,0:T(8,128)(2,1)}), bf16[4,8,128,128]{3,2,1,0:T(8,128)(2,1)S(1)}, u32[]{:S(2)}, u32[]{:S(2)}) async-start(bf16[4,8,128,128]{3,2,1,0:T(8,128)(2,1)} %stack.2), calls=%async_computation | async-start | bytes 2097152 | tf_op jit(solution)/shard_map/all_to_all | solution.py:69
  18.5 13.4 %all-to-all-done = bf16[4,8,128,128]{3,2,1,0:T(8,128)(2,1)S(1)} async-done(((bf16[4,8,128,128]{3,2,1,0:T(8,128)(2,1)}), bf16[4,8,128,128]{3,2,1,0:T(8,128)(2,1)S(1)}, u32[]{:S(2)}, u32[]{:S(2)}) %all-to-all-start) | async-done | bytes 1048608 | tf_op jit(solution)/shard_map/all_to_all | solution.py:69
  31.8 32.9 %all-gather.5.cloned.1.call-done = bf16[32,512,128]{2,1,0:T(8,128)(2,1)} async-done(((bf16[8,512,128]{2,1,0:T(8,128)(2,1)}), bf16[32,512,128]{2,1,0:T(8,128)(2,1)}) %all-gather.5.cloned.1.call-update) | async-done | bytes 4194320 | tf_op jit(solution)/shard_map/all_gather | solution.py:67
  64.8 44.2 %while.10 = (s32[]{:T(128)}, f32[8,128,128]{2,1,0:T(8,128)}, bf16[8,32]{1,0:T(8,128)(2,1)S(1)}, bf16[8,512,128]{2,1,0:T(8,128)(2,1)}, bf16[32,512,128]{2,1,0:T(8...) while((s32[]{:T(128)}, f32[8,128,128]{2,1,0:T(8,128)}, bf16[8,32]{1,0:T(8,128)(2,1)S(1)}, ...), condition=%wide.region_2.3_spmd, body=%wide.region_1.2_spmd.sunk | while | flops 807403520 | bytes 9766481 | solution.py:56
  64.8 3.0 %fusion.45 = bf16[32,128,128]{2,1,0:T(8,128)(2,1)S(1)} fusion(bf16[32,512,128]{2,1,0:T(8,128)(2,1)} %get-tuple-element.129, bf16[8,512,128]{2,1,0:T(8,128)(2,1)} %get-tuple-element.128, s32[]{:T(128)} %get-tuple-element.118), kind=kOutput, calls=%fused_computation.4.clone.1 | convolution fusion | flops 537395200 | bytes 5374464 | tf_op jit(solution)/shard_map/while/body/eval_jaxpr/ra,crb->cab/dot_general | solution.py:45
  67.8 1.2 fusion.46
  70.3 3.0 %fusion.45 = bf16[32,128,128]{2,1,0:T(8,128)(2,1)S(1)} fusion(bf16[32,512,128]{2,1,0:T(8,128)(2,1)} %get-tuple-element.129, bf16[8,512,128]{2,1,0:T(8,128)(2,1)} %get-tuple-element.128, s32[]{:T(128)} %get-tuple-element.118), kind=kOutput, calls=%fused_computation.4.clone.1 | convolution fusion | flops 537395200 | bytes 5374464 | tf_op jit(solution)/shard_map/while/body/eval_jaxpr/ra,crb->cab/dot_general | solution.py:45
  73.3 1.2 fusion.46
  75.7 3.3 %fusion.45 = bf16[32,128,128]{2,1,0:T(8,128)(2,1)S(1)} fusion(bf16[32,512,128]{2,1,0:T(8,128)(2,1)} %get-tuple-element.129, bf16[8,512,128]{2,1,0:T(8,128)(2,1)} %get-tuple-element.128, s32[]{:T(128)} %get-tuple-element.118), kind=kOutput, calls=%fused_computation.4.clone.1 | convolution fusion | flops 537395200 | bytes 5374464 | tf_op jit(solution)/shard_map/while/body/eval_jaxpr/ra,crb->cab/dot_general | solution.py:45
  79.1 1.2 fusion.46
  81.5 3.0 %fusion.45 = bf16[32,128,128]{2,1,0:T(8,128)(2,1)S(1)} fusion(bf16[32,512,128]{2,1,0:T(8,128)(2,1)} %get-tuple-element.129, bf16[8,512,128]{2,1,0:T(8,128)(2,1)} %get-tuple-element.128, s32[]{:T(128)} %get-tuple-element.118), kind=kOutput, calls=%fused_computation.4.clone.1 | convolution fusion | flops 537395200 | bytes 5374464 | tf_op jit(solution)/shard_map/while/body/eval_jaxpr/ra,crb->cab/dot_general | solution.py:45
  84.6 1.2 fusion.46
  87.0 3.1 %fusion.45 = bf16[32,128,128]{2,1,0:T(8,128)(2,1)S(1)} fusion(bf16[32,512,128]{2,1,0:T(8,128)(2,1)} %get-tuple-element.129, bf16[8,512,128]{2,1,0:T(8,128)(2,1)} %get-tuple-element.128, s32[]{:T(128)} %get-tuple-element.118), kind=kOutput, calls=%fused_computation.4.clone.1 | convolution fusion | flops 537395200 | bytes 5374464 | tf_op jit(solution)/shard_map/while/body/eval_jaxpr/ra,crb->cab/dot_general | solution.py:45
  92.6 3.0 %fusion.45 = bf16[32,128,128]{2,1,0:T(8,128)(2,1)S(1)} fusion(bf16[32,512,128]{2,1,0:T(8,128)(2,1)} %get-tuple-element.129, bf16[8,512,128]{2,1,0:T(8,128)(2,1)} %get-tuple-element.128, s32[]{:T(128)} %get-tuple-element.118), kind=kOutput, calls=%fused_computation.4.clone.1 | convolution fusion | flops 537395200 | bytes 5374464 | tf_op jit(solution)/shard_map/while/body/eval_jaxpr/ra,crb->cab/dot_general | solution.py:45
  95.6 1.2 fusion.46
  98.1 3.0 %fusion.45 = bf16[32,128,128]{2,1,0:T(8,128)(2,1)S(1)} fusion(bf16[32,512,128]{2,1,0:T(8,128)(2,1)} %get-tuple-element.129, bf16[8,512,128]{2,1,0:T(8,128)(2,1)} %get-tuple-element.128, s32[]{:T(128)} %get-tuple-element.118), kind=kOutput, calls=%fused_computation.4.clone.1 | convolution fusion | flops 537395200 | bytes 5374464 | tf_op jit(solution)/shard_map/while/body/eval_jaxpr/ra,crb->cab/dot_general | solution.py:45
  103.5 3.0 %fusion.45 = bf16[32,128,128]{2,1,0:T(8,128)(2,1)S(1)} fusion(bf16[32,512,128]{2,1,0:T(8,128)(2,1)} %get-tuple-element.129, bf16[8,512,128]{2,1,0:T(8,128)(2,1)} %get-tuple-element.128, s32[]{:T(128)} %get-tuple-element.118), kind=kOutput, calls=%fused_computation.4.clone.1 | convolution fusion | flops 537395200 | bytes 5374464 | tf_op jit(solution)/shard_map/while/body/eval_jaxpr/ra,crb->cab/dot_general | solution.py:45
  106.5 1.2 fusion.46
  109.0 31.3 %all-gather.3.cloned.1.call-done = bf16[32,512,512]{2,1,0:T(8,128)(2,1)} async-done(((bf16[1,512,512]{2,1,0:T(8,128)(2,1)}), bf16[32,512,512]{2,1,0:T(8,128)(2,1)}) %all-gather.3.cloned.1.call-update) | async-done | bytes 16777232 | tf_op jit(solution)/shard_map/all_gather | solution.py:73
  140.3 20.3 %fusion.11 = bf16[16,512,512]{2,0,1:T(8,128)(2,1)} fusion(bf16[32,512,512]{2,1,0:T(8,128)(2,1)} %all-gather.3.cloned.1.call-done, s32[16]{0:T(128)S(1)} %select_reduce_fusion), kind=kOutput, calls=%fused_computation.14 | convolution fusion | flops 272630272 | bytes 25165888 | tf_op jit(solution)/shard_map/sk,kxn->sxn/dot_general | solution.py:21
  160.6 11.7 %copy.34 = bf16[16,512,512]{2,1,0:T(8,128)(2,1)} copy(bf16[16,512,512]{2,0,1:T(8,128)(2,1)} %fusion.11) | data formatting | bytes 16777216 | tf_op jit(solution)/shard_map/reshape | solution.py:74
  172.3 5.8 %convolution_convert_fusion.2 = bf16[8,2,512,128]{3,2,1,0:T(8,128)(2,1)S(1)} fusion(bf16[8,2,512,512]{3,2,1,0:T(8,128)(2,1)} %bitcast.57, bf16[8,512,128]{2,1,0:T(8,128)(2,1)S(1)} %copy-done), kind=kOutput, calls=%fused_computation.15 | convolution fusion | flops 1074790400 | bytes 11534336 | tf_op jit(solution)/shard_map/pkxn,pnq->pkxq/dot_general | solution.py:75
  178.1 1.3 fusion.14
  (33 shorter events, 17.5 us)
Async XLA Ops:
  6.5 58.2 %all-gather.5.cloned.1.call-start = ((), (), s32[]{:S(2)}) async-start(), calls=%async_computation.2 | async-start | bytes 5242880 | tf_op jit(solution)/shard_map/all_gather | solution.py:67
  7.3 133.1 %all-gather.3.cloned.1.call-start = ((), (), s32[]{:S(2)}) async-start(), calls=%async_computation.1 | async-start | bytes 17301504 | tf_op jit(solution)/shard_map/all_gather | solution.py:73
  10.2 21.7 %all-to-all-start = ((bf16[4,8,128,128]{3,2,1,0:T(8,128)(2,1)}), bf16[4,8,128,128]{3,2,1,0:T(8,128)(2,1)S(1)}, u32[]{:S(2)}, u32[]{:S(2)}) async-start(bf16[4,8,128,128]{3,2,1,0:T(8,128)(2,1)} %stack.2), calls=%async_computation | async-start | bytes 2097152 | tf_op jit(solution)/shard_map/all_to_all | solution.py:69
  160.6 11.7 %copy-start = (bf16[8,512,128]{2,1,0:T(8,128)(2,1)S(1)}, bf16[8,512,128]{2,1,0:T(8,128)(2,1)}, u32[]{:S(2)}) copy-start(bf16[8,512,128]{2,1,0:T(8,128)(2,1)} %get-tuple-element.139) | copy-start | bytes 3145732
  172.3 5.8 %copy-start.1 = (f32[8,128,128]{2,1,0:T(8,128)S(1)}, f32[8,128,128]{2,1,0:T(8,128)}, u32[]{:S(2)}) copy-start(f32[8,128,128]{2,1,0:T(8,128)} %get-tuple-element.37) | copy-start | bytes 1572868
Sparse Core Ops, SparseCore 0:
  9.0 55.7 all-gather.4
  67.0 73.2 all-gather.2
